TPU v7x, 128 devices: a whole 4x4x4 slice. The times are simulated.
128 devices in a mesh: seq: 16 (over y_lo, x, core), tp: 8 (over y_hi, z).
Axes of the slice: x: 4, y: 4 (y_hi: 2, y_lo: 2; y = y_hi * 2 + y_lo), z: 4, core: 2. Of those that a mesh axis runs over, the one named last changes fastest.
Arguments:
- queries: bfloat16 [8192, 6144], P('seq', 'tp'), may hold values from -6 to 6
- keys: bfloat16 [8192, 1024], P('seq', 'tp'), may hold values from -6 to 6
- values: bfloat16 [8192, 1024], P('seq', 'tp'), may hold values from -6 to 6
- segment_ids: int32 [8192], replicated, may hold values from 0 to 7, never falling along the last dimension, each value on 1 to 6144 neighbouring positions
- packing: int32 [64, 2], replicated, may hold values from 0 to 15, as said below
- out_weight: bfloat16 [6144, 12288], P('tp', 'seq'), may hold values from -0.625 to 0.625
Outputs:
- attended: bfloat16 [8192, 12288], P('seq', 'tp')
Inputs may be any that keep to these rules, and one draw needn't show every extreme that they name: `packing`: each arriving block gets a distinct packed place, so every packed shard receives exactly 4 blocks at offsets 0 to 3; the blocks of one shard go to 4 different packed shards. `segment_ids`: document ids never fall along the tokens; each document has 1 to 6144 tokens and one has exactly 6144.
All inputs are finite; a program needn't handle non-finite values.
Results may differ from a plain program's by a relative error of at most 0.015.
Values may be sent and summed in bfloat16 or wider, within the bound.
A program may use at most 128 MiB of HBM per device.

v0:
```python
import functools
import math
import jax
import jax.numpy as jnp
from jax import lax
from jax.sharding import Mesh, PartitionSpec as P

HEAD_DIM = 128
WINDOW = 4096
BLOCK = 128
SEQ = ("ylo", "x", "c")
TP = ("yhi", "z")


def attend_head(q_rows, k_rows, v_rows, q_pos, k_pos, q_seg, k_seg):
    scores = lax.dot_general(
        q_rows, k_rows, (((1,), (1,)), ((), ())), preferred_element_type=jnp.float32
    )
    scores = scores * (1.0 / math.sqrt(HEAD_DIM))
    allowed = (k_pos[None, :] <= q_pos[:, None]) & (k_pos[None, :] > q_pos[:, None] - WINDOW)
    allowed = allowed & (k_seg[None, :] == q_seg[:, None])
    scores = jnp.where(allowed, scores, -jnp.inf)
    top_score = jnp.max(scores, axis=1, keepdims=True)
    expo = jnp.exp(scores - top_score)
    weights = (expo / jnp.sum(expo, axis=1, keepdims=True)).astype(jnp.bfloat16)
    return jnp.dot(weights, v_rows, preferred_element_type=jnp.float32).astype(jnp.bfloat16)


def shards(seq_count, queries, keys, values, segment_ids, packing, out_weight):
    tok_rows = queries.shape[0]
    q_cols = queries.shape[1]
    kv_cols = keys.shape[1]
    shard_index = lax.axis_index(SEQ)
    per_shard = tok_rows // BLOCK
    blocks_all = packing.shape[0]
    kv_local = jnp.concatenate([keys, values], axis=1)
    kv_all = lax.all_gather(kv_local, SEQ, axis=0, tiled=True)
    kv_blocks = kv_all.reshape(blocks_all, BLOCK, 2 * kv_cols)
    target = packing[:, 0] * per_shard + packing[:, 1]
    source = (
        jnp.zeros((blocks_all,), jnp.int32).at[target].set(jnp.arange(blocks_all, dtype=jnp.int32))
    )
    span_blocks = WINDOW // BLOCK
    ctx_blocks = span_blocks + per_shard
    blk_ids = shard_index * per_shard - span_blocks + jnp.arange(ctx_blocks, dtype=jnp.int32)
    src = jnp.take(source, jnp.clip(blk_ids, 0, blocks_all - 1))
    context = jnp.take(kv_blocks, src, axis=0).reshape(ctx_blocks * BLOCK, 2 * kv_cols)
    own_blocks = queries.reshape(per_shard, BLOCK, q_cols)
    own_list = lax.dynamic_slice_in_dim(packing, shard_index * per_shard, per_shard, 0)
    slot_ids = jnp.arange(seq_count, dtype=jnp.int32)
    routing = (own_list[:, 0][None, :] == slot_ids[:, None]).astype(jnp.bfloat16)
    outgoing = jnp.einsum(
        "db,brc->drc", routing, own_blocks, preferred_element_type=jnp.float32
    ).astype(jnp.bfloat16)
    incoming = lax.all_to_all(outgoing, SEQ, split_axis=0, concat_axis=0, tiled=True)
    arriving = packing[:, 0] == shard_index
    offset_ids = jnp.arange(per_shard, dtype=jnp.int32)
    at_offset = ((packing[:, 1][None, :] == offset_ids[:, None]) & arriving[None, :]).astype(
        jnp.float32
    )
    senders = jnp.arange(blocks_all, dtype=jnp.int32) // per_shard
    from_sender = (senders[:, None] == slot_ids[None, :]).astype(jnp.float32)
    placing = jnp.dot(at_offset, from_sender, precision=lax.Precision.HIGHEST).astype(jnp.bfloat16)
    packed = jnp.einsum(
        "od,drc->orc", placing, incoming, preferred_element_type=jnp.float32
    ).astype(jnp.bfloat16)
    queries_here = packed.reshape(tok_rows, q_cols)
    w_swapped = lax.ppermute(out_weight, ("ylo", "yhi"), perm=[(0, 0), (1, 2), (2, 1), (3, 3)])
    w_cols = lax.all_gather(w_swapped, "x", axis=1, tiled=True)
    w_here = lax.all_gather(w_cols, "ylo", axis=0, tiled=True)
    context, w_here = lax.optimization_barrier((context, w_here))
    ctx_keys = context[:, :kv_cols]
    ctx_values = context[:, kv_cols:]
    ctx_rows = context.shape[0]
    q_pos = shard_index * tok_rows + jnp.arange(tok_rows, dtype=jnp.int32)
    k_pos = shard_index * tok_rows - WINDOW + jnp.arange(ctx_rows, dtype=jnp.int32)
    padded_seg = jnp.concatenate([jnp.full((WINDOW,), -1, jnp.int32), segment_ids], axis=0)
    q_seg = lax.dynamic_slice_in_dim(segment_ids, shard_index * tok_rows, tok_rows, 0)
    k_seg = lax.dynamic_slice_in_dim(padded_seg, shard_index * tok_rows, ctx_rows, 0)
    heads_here = q_cols // HEAD_DIM

    def one_head(head_index):
        q_head = lax.dynamic_slice_in_dim(queries_here, head_index * HEAD_DIM, HEAD_DIM, 1)
        return attend_head(q_head, ctx_keys, ctx_values, q_pos, k_pos, q_seg, k_seg)

    per_head = lax.map(one_head, jnp.arange(heads_here, dtype=jnp.int32))
    attended = jnp.transpose(per_head, (1, 0, 2)).reshape(tok_rows, q_cols)
    h_groups = lax.all_gather(attended, "yhi", axis=1, tiled=True)
    h_here = lax.all_gather(h_groups, "c", axis=0, tiled=True)
    part = jnp.dot(h_here, w_here, preferred_element_type=jnp.float32).astype(jnp.bfloat16)
    summed = lax.psum_scatter(part, "z", scatter_dimension=1, tiled=True)
    swapped = lax.all_to_all(summed, "c", split_axis=0, concat_axis=0, tiled=True)
    return jnp.concatenate([swapped[:tok_rows], swapped[tok_rows:]], axis=1)


def solution(mesh):
    seq_count, tp_count = mesh.devices.shape
    fine = Mesh(mesh.devices.reshape(2, seq_count // 4, 2, 2, tp_count // 2), SEQ + TP)
    in_specs = (P(SEQ, TP), P(SEQ, TP), P(SEQ, TP), P(), P(), P(TP, SEQ))
    out_specs = P(SEQ, TP)
    return jax.shard_map(
        functools.partial(shards, seq_count),
        mesh=fine,
        in_specs=in_specs,
        out_specs=out_specs,
        check_vma=False,
    )
```

profile of v0, /device:TPU:1, one launch (start us, length us, event | category | flops | bytes accessed | tf_op | source)
XLA Modules:
  0.0 490.7 jit_solution(2651547205642408613)
XLA Ops:
  11.5 82.0 %all-gather.8.cloned.1.call-done = bf16[768,3072]{1,0:T(8,128)(2,1)} async-done(((bf16[768,768]{1,0:T(8,128)(2,1)}), bf16[768,3072]{1,0:T(8,128)(2,1)}) %all-gather.8.cloned.1.call-update) | async-done | bytes 4718608 | tf_op jit(solution)/shard_map/all_gather | solution.py:69
  95.0 2.7 copy.10
  97.7 5.2 %all-to-all-start = ((bf16[16,128,768]{2,1,0:T(8,128)(2,1)}), bf16[16,128,768]{2,1,0:T(8,128)(2,1)S(1)}, u32[]{:S(2)}, u32[]{:S(2)}) async-start(bf16[16,128,768]{2,1,0:T(8,128)(2,1)} %copy.10), calls=%async_computation | async-start | bytes 6291456 | tf_op jit(solution)/shard_map/all_to_all | solution.py:55
  105.9 48.2 %all-to-all-done = bf16[16,128,768]{2,1,0:T(8,128)(2,1)S(1)} async-done(((bf16[16,128,768]{2,1,0:T(8,128)(2,1)}), bf16[16,128,768]{2,1,0:T(8,128)(2,1)S(1)}, u32[]{:S(2)}, u32[]{:S(2)}) %all-to-all-start) | async-done | bytes 3145760 | tf_op jit(solution)/shard_map/all_to_all | solution.py:55
  156.9 7.8 %all-gather.6.cloned.1.call-done = bf16[8192,256]{1,0:T(8,128)(2,1)} async-done(((bf16[512,256]{1,0:T(8,128)(2,1)}), bf16[8192,256]{1,0:T(8,128)(2,1)}) %all-gather.6.cloned.1.call-update) | async-done | bytes 4194320 | tf_op jit(solution)/shard_map/all_gather | solution.py:37
  164.7 4.4 gather_fusion.1
  169.1 3.8 bitcast_select_fusion
  173.0 113.7 %all-gather.10.cloned.1.call-done = bf16[1536,3072]{1,0:T(8,128)(2,1)} async-done(((bf16[768,3072]{1,0:T(8,128)(2,1)}), bf16[1536,3072]{1,0:T(8,128)(2,1)}) %all-gather.10.cloned.1.call-update) | async-done | bytes 9437200 | tf_op jit(solution)/shard_map/all_gather | solution.py:70
  287.8 59.0 %while.13 = (s32[]{:T(128)}, bf16[6,512,128]{1,2,0:T(8,128)(2,1)}, s32[4608]{0:T(1024)}, s32[512]{0:T(512)S(1)}, s32[6]{0:T(128)S(1)}, /*index=5*/bf16[512,768]{...) while((s32[]{:T(128)}, bf16[6,512,128]{1,2,0:T(8,128)(2,1)}, ...), condition=%wide.region_4.5_spmd.clone, body=%wide.region_1.0_spmd.clone.sunk | while | flops 1238700544 | bytes 31535820 | solution.py:86
  289.0 4.2 fusion.44
  294.6 2.2 fusion.46
  298.8 4.2 fusion.44
  304.4 2.2 fusion.46
  308.6 4.2 fusion.44
  314.3 2.2 fusion.46
  318.5 4.2 fusion.44
  328.3 4.2 fusion.44
  333.9 2.2 fusion.46
  338.1 4.2 fusion.44
  346.8 32.3 %all-gather.12.cloned.1.call-done = bf16[512,1536]{0,1:T(8,128)(2,1)} async-done(((bf16[512,768]{0,1:T(8,128)(2,1)}), bf16[512,1536]{0,1:T(8,128)(2,1)}) %all-gather.12.cloned.1.call-update) | async-done | bytes 1572880 | tf_op jit(solution)/shard_map/all_gather | solution.py:88
  379.5 15.9 %all-gather.14.cloned.1.call-done = bf16[1024,1536]{0,1:T(8,128)(2,1)} async-done(((bf16[512,1536]{0,1:T(8,128)(2,1)}), bf16[1024,1536]{0,1:T(8,128)(2,1)}) %all-gather.14.cloned.1.call-update) | async-done | bytes 3145744 | tf_op jit(solution)/shard_map/all_gather | solution.py:89
  395.4 15.3 %convolution_convert_fusion = bf16[1024,3072]{1,0:T(8,128)(2,1)} fusion(bf16[1024,1536]{0,1:T(8,128)(2,1)} %all-gather.14.cloned.1.call-done, bf16[1536,3072]{1,0:T(8,128)(2,1)} %all-gather.10.cloned.1.call-done), kind=kOutput, calls=%fused_computation.18 | convolution fusion | flops 9666822144 | bytes 18874368 | tf_op jit(solution)/shard_map/dot_general | solution.py:90
  410.7 65.3 %reduce-scatter.2.cloned.1.call-done = bf16[1024,768]{1,0:T(8,128)(2,1)} async-done(((bf16[1024,3072]{1,0:T(8,128)(2,1)}), bf16[1024,768]{1,0:T(8,128)(2,1)}) %reduce-scatter.2.cloned.1.call-update) | async-done | bytes 1572880 | tf_op jit(solution)/shard_map/reduce_scatter | solution.py:91
  476.0 6.5 %all_to_all.14 = bf16[2,512,768]{2,1,0:T(8,128)(2,1)S(1)} all-to-all(bf16[2,512,768]{2,1,0:T(8,128)(2,1)} %bitcast.53), channel_id=1, replica_groups=mesh['ylo'=2,'x'=4,'c'=2,'yhi'=2,'z'=4] {'c'}, dimensions={0} | all-to-all | bytes 3145728 | tf_op jit(solution)/shard_map/all_to_all | solution.py:92
  (88 shorter events, 36.2 us)
Async XLA Ops:
  6.5 87.0 %copy-start = (bf16[512,768]{1,0:T(8,128)(2,1)S(1)}, bf16[512,768]{1,0:T(8,128)(2,1)}, u32[]{:S(2)}) copy-start(bf16[512,768]{1,0:T(8,128)(2,1)} %param.8) | copy-start | bytes 2359300
  6.5 86.9 %all-gather.8.cloned.1.call-start = ((), (), s32[]{:S(2)}) async-start(), calls=%async_computation.4 | async-start | bytes 5898240 | tf_op jit(solution)/shard_map/all_gather | solution.py:69
  6.5 2.1 collective-permute-start
  8.6 1.0 copy-start.2
  8.6 84.9 %copy-start.4 = (s32[64,2]{0,1:T(2,128)S(1)}, s32[64,2]{0,1:T(2,128)}, u32[]{:S(2)}) copy-start(s32[64,2]{0,1:T(2,128)} %param.12) | copy-start | bytes 1540
  9.6 155.1 %all-gather.6.cloned.1.call-start = ((), (), s32[]{:S(2)}) async-start(), calls=%async_computation.3 | async-start | bytes 4456448 | tf_op jit(solution)/shard_map/all_gather | solution.py:37
  11.4 275.2 %all-gather.10.cloned.1.call-start = ((), (), s32[]{:S(2)}) async-start(), calls=%async_computation.5 | async-start | bytes 14155776 | tf_op jit(solution)/shard_map/all_gather | solution.py:70
  97.7 7.1 %copy-start.3 = (s32[8192]{0:T(1024)S(1)}, s32[8192]{0:T(1024)}, u32[]{:S(2)}) copy-start(s32[8192]{0:T(1024)} %param.11) | copy-start | bytes 98308
  97.7 56.3 %all-to-all-start = ((bf16[16,128,768]{2,1,0:T(8,128)(2,1)}), bf16[16,128,768]{2,1,0:T(8,128)(2,1)S(1)}, u32[]{:S(2)}, u32[]{:S(2)}) async-start(bf16[16,128,768]{2,1,0:T(8,128)(2,1)} %copy.10), calls=%async_computation | async-start | bytes 6291456 | tf_op jit(solution)/shard_map/all_to_all | solution.py:55
  102.9 276.2 %all-gather.12.cloned.1.call-start = ((), (), s32[]{:S(2)}) async-start(), calls=%async_computation.6 | async-start | bytes 2359296 | tf_op jit(solution)/shard_map/all_gather | solution.py:88
  346.8 48.6 %all-gather.14.cloned.1.call-start = ((), (), s32[]{:S(2)}) async-start(), calls=%async_computation.7 | async-start | bytes 4718592 | tf_op jit(solution)/shard_map/all_gather | solution.py:89
  379.2 96.8 %reduce-scatter.2.cloned.1.call-start = ((), (), s32[]{:S(2)}) async-start(), calls=%async_computation.8 | async-start | bytes 7864320 | tf_op jit(solution)/shard_map/reduce_scatter | solution.py:91
  476.0 7.9 %copy-start.1 = (bf16[512,768]{1,0:T(8,128)(2,1)S(1)}, bf16[512,768]{1,0:T(8,128)(2,1)}, u32[]{:S(2)}) copy-start(bf16[512,768]{1,0:T(8,128)(2,1)} %param.8) | copy-start | bytes 2359300
Sparse Core Ops, SparseCore 0:
  9.8 83.6 all-gather.7
  95.1 69.5 all-gather.5
  166.4 120.2 all-gather.9
  346.9 32.2 all-gather.11
  380.7 14.6 all-gather.13
  410.8 65.1 reduce-scatter.1
where the time goes:
time: 491 us
  waiting for transfers between devices  365 us (74%)
  matrix products  57.6 us (12%)
  local copies, waits for them, and re-layouts  21.2 us (4%)
  other arithmetic  15.4 us (3%)
  between operations  13.6 us (3%)
  starting transfers between devices  7.67 us (2%)
  blocking collectives  6.54 us (1%)
    all_gather x1, waiting for transfers between devices, shards(): w_here = lax.all_gather(w_cols, 'ylo', axis=0, tiled=True)  114 us
    all_gather x1, waiting for transfers between devices, shards(): w_cols = lax.all_gather(w_swapped, 'x', axis=1, tiled=True)  82 us
    reduce_scatter x1, waiting for transfers between devices, shards(): summed = lax.psum_scatter(part, 'z', scatter_dimension=1, tiled=True)  65.3 us
    all_to_all x1, waiting for transfers between devices, shards(): lax.all_to_all(outgoing, SEQ, split_axis=0, concat_axis=0, tiled=True)  48.2 us
    all_gather x1, waiting for transfers between devices, shards(): h_groups = lax.all_gather(attended, 'yhi', axis=1, tiled=True)  32.3 us
    dot_general x6, matrix products, attend_head(): lax.dot_general(q_rows, k_rows, (((1,), (1,)), ((), ())), preferred_eleme...  25.4 us
    all_gather x1, waiting for transfers between devices, shards(): h_here = lax.all_gather(h_groups, 'c', axis=0, tiled=True)  15.9 us
    dot_general x1, matrix products, shards(): jnp.dot(h_here, w_here, preferred_element_type=jnp.float32)  15.3 us
  transfers between devices with their start and end apart: 8, of which 7 were waited for; matrix products, arithmetic and copies ran while one was open for 4% of the time, Pallas kernels for 0%

commit v1 on v0

--- a/solution.py
+++ b/solution.py
@@ -67,7 +67,16 @@
     queries_here = packed.reshape(tok_rows, q_cols)
     w_swapped = lax.ppermute(out_weight, ("ylo", "yhi"), perm=[(0, 0), (1, 2), (2, 1), (3, 3)])
     w_cols = lax.all_gather(w_swapped, "x", axis=1, tiled=True)
-    w_here = lax.all_gather(w_cols, "ylo", axis=0, tiled=True)
+    fill_page = lambda frame_in, across: jnp.concatenate(
+        lax.all_to_all(
+            jnp.stack([frame_in] * lax.axis_size(across), axis=0),
+            axis_name=across,
+            split_axis=0,
+            concat_axis=0,
+        ),
+        0,
+    )
+    w_here = fill_page(w_cols, "ylo")
     context, w_here = lax.optimization_barrier((context, w_here))
     ctx_keys = context[:, :kv_cols]
     ctx_values = context[:, kv_cols:]

time: 491 us -> 466 us (0.949)
  waiting for transfers between devices: 365 us -> 291 us
  starting transfers between devices: 7.67 us -> 44.6 us
  other arithmetic: 15.4 us -> 23.6 us
    all_gather x1 -> x0, waiting for transfers between devices: 114 us -> none  [shards(): w_here = lax.all_gather(w_cols, 'ylo', axis=0, tiled=True)]
    all_to_all x0 -> x1, waiting for transfers between devices: none -> 76 us  [shards(): lax.all_to_all(jnp.stack([frame_in] * lax.axis_size(across), axis=0), axi...]
    all_to_all x1, waiting for transfers between devices: 48.2 us -> 0.01 us  [shards(): lax.all_to_all(outgoing, SEQ, split_axis=0, concat_axis=0, tiled=True)]
    all_to_all x1, starting transfers between devices: 5.2 us -> 34.7 us  [shards(): lax.all_to_all(outgoing, SEQ, split_axis=0, concat_axis=0, tiled=True)]
    all_gather x1, waiting for transfers between devices: 7.77 us -> 26.6 us  [shards(): kv_all = lax.all_gather(kv_local, SEQ, axis=0, tiled=True)]
    another operation x0 -> x1, other arithmetic: none -> 8.29 us  [shards(): jnp.stack([frame_in] * lax.axis_size(across), axis=0)]
    all_to_all x0 -> x1, starting transfers between devices: none -> 7.46 us  [shards(): lax.all_to_all(jnp.stack([frame_in] * lax.axis_size(across), axis=0), axi...]
    all_gather x1, waiting for transfers between devices: 82 us -> 76 us  [shards(): w_cols = lax.all_gather(w_swapped, 'x', axis=1, tiled=True)]
  transfers between devices with their start and end apart: 8 -> 8, of which waited for: 7 -> 6; matrix products, arithmetic and copies ran while one was open for 4% -> 7% of each run, Pallas kernels for 0% -> 0%
where the time goes in v1:
time: 466 us; the launch traced here: 465 us
  waiting for transfers between devices  291 us (62%)
  matrix products  60.1 us (13%)
  starting transfers between devices  44.6 us (10%)
  other arithmetic  23.6 us (5%)
  local copies, waits for them, and re-layouts  21.8 us (5%)
  between operations  13.3 us (3%)
  blocking collectives  6.51 us (1%)
    all_to_all x1, waiting for transfers between devices, shards(): lax.all_to_all(jnp.stack([frame_in] * lax.axis_size(across), axis=0), axi...  76 us
    all_gather x1, waiting for transfers between devices, shards(): w_cols = lax.all_gather(w_swapped, 'x', axis=1, tiled=True)  76 us
    reduce_scatter x1, waiting for transfers between devices, shards(): summed = lax.psum_scatter(part, 'z', scatter_dimension=1, tiled=True)  65.3 us
    all_to_all x1, starting transfers between devices, shards(): lax.all_to_all(outgoing, SEQ, split_axis=0, concat_axis=0, tiled=True)  34.7 us
    all_gather x1, waiting for transfers between devices, shards(): h_groups = lax.all_gather(attended, 'yhi', axis=1, tiled=True)  31.5 us
    all_gather x1, waiting for transfers between devices, shards(): kv_all = lax.all_gather(kv_local, SEQ, axis=0, tiled=True)  26.6 us
    dot_general x6, matrix products, attend_head(): lax.dot_general(q_rows, k_rows, (((1,), (1,)), ((), ())), preferred_eleme...  25.9 us
    all_gather x1, waiting for transfers between devices, shards(): h_here = lax.all_gather(h_groups, 'c', axis=0, tiled=True)  15.9 us
  transfers between devices with their start and end apart: 8, of which 6 were waited for; matrix products, arithmetic and copies ran while one was open for 7% of the time, Pallas kernels for 0%

profile of v1, /device:TPU:1, one launch (start us, length us, event | category | flops | bytes accessed | tf_op | source)
XLA Modules:
  0.0 464.9 jit_solution(18154866162071020420)
XLA Ops:
  13.7 2.7 copy.10
  16.3 34.7 %all-to-all-start = ((bf16[16,128,768]{2,1,0:T(8,128)(2,1)}), bf16[16,128,768]{2,1,0:T(8,128)(2,1)}, u32[]{:S(2)}, u32[]{:S(2)}) async-start(bf16[16,128,768]{2,1,0:T(8,128)(2,1)} %copy.10), calls=%async_computation | async-start | bytes 6291456 | tf_op jit(solution)/shard_map/all_to_all | solution.py:55
  51.0 76.0 %all-gather.7.cloned.1.call-done = bf16[768,3072]{1,0:T(8,128)(2,1)} async-done(((bf16[768,768]{1,0:T(8,128)(2,1)}), bf16[768,3072]{1,0:T(8,128)(2,1)}) %all-gather.7.cloned.1.call-update) | async-done | bytes 4718608 | tf_op jit(solution)/shard_map/all_gather | solution.py:69
  127.0 8.3 %pad_maximum_fusion = bf16[2,768,3072]{2,1,0:T(8,128)(2,1)} fusion(bf16[1,768,3072]{2,1,0:T(8,128)(2,1)} %bitcast.55), kind=kLoop, calls=%fused_computation.18 | loop fusion | flops 4718592 | bytes 14155776 | tf_op jit(solution)/shard_map/stack | solution.py:72
  135.3 7.5 %all-to-all-start.1 = ((bf16[2,768,3072]{2,1,0:T(8,128)(2,1)}), bf16[2,768,3072]{2,1,0:T(8,128)(2,1)}, u32[]{:S(2)}, u32[]{:S(2)}) async-start(bf16[2,768,3072]{2,1,0:T(8,128)(2,1)} %pad_maximum_fusion), calls=%async_computation.1 | async-start | bytes 18874368 | tf_op jit(solution)/shard_map/all_to_all | solution.py:71
  145.2 3.9 fusion.12
  150.1 26.6 %all-gather.5.cloned.1.call-done = bf16[8192,256]{1,0:T(8,128)(2,1)} async-done(((bf16[512,256]{1,0:T(8,128)(2,1)}), bf16[8192,256]{1,0:T(8,128)(2,1)}) %all-gather.5.cloned.1.call-update) | async-done | bytes 4194320 | tf_op jit(solution)/shard_map/all_gather | solution.py:37
  176.7 4.5 gather_fusion.1
  181.2 3.8 bitcast_select_fusion
  185.0 76.0 %all-to-all-done.1 = bf16[2,768,3072]{2,1,0:T(8,128)(2,1)} async-done(((bf16[2,768,3072]{2,1,0:T(8,128)(2,1)}), bf16[2,768,3072]{2,1,0:T(8,128)(2,1)}, u32[]{:S(2)}, u32[]{:S(2)}) %all-to-all-start.1) | async-done | bytes 9437216 | tf_op jit(solution)/shard_map/all_to_all | solution.py:71
  262.6 59.5 %while.13 = (s32[]{:T(128)}, bf16[6,512,128]{1,2,0:T(8,128)(2,1)}, s32[4608]{0:T(1024)S(1)}, s32[512]{0:T(512)S(1)}, s32[6]{0:T(128)S(1)}, /*index=5*/bf16[512,7...) while((s32[]{:T(128)}, bf16[6,512,128]{1,2,0:T(8,128)(2,1)}, ...), condition=%wide.region_4.5_spmd.clone, body=%wide.region_1.0_spmd.clone.sunk | while | flops 1238700544 | bytes 36252392 | solution.py:95
  263.8 4.3 fusion.44
  269.5 2.2 fusion.46
  273.7 4.3 fusion.44
  283.6 4.3 fusion.44
  289.4 2.2 fusion.46
  293.5 4.3 fusion.44
  303.5 4.3 fusion.44
  313.4 4.3 fusion.44
  322.2 31.5 %all-gather.9.cloned.1.call-done = bf16[512,1536]{0,1:T(8,128)(2,1)} async-done(((bf16[512,768]{0,1:T(8,128)(2,1)}), bf16[512,1536]{0,1:T(8,128)(2,1)}) %all-gather.9.cloned.1.call-update) | async-done | bytes 1572880 | tf_op jit(solution)/shard_map/all_gather | solution.py:97
  354.0 15.9 %all-gather.11.cloned.1.call-done = bf16[1024,1536]{0,1:T(8,128)(2,1)} async-done(((bf16[512,1536]{0,1:T(8,128)(2,1)}), bf16[1024,1536]{0,1:T(8,128)(2,1)}) %all-gather.11.cloned.1.call-update) | async-done | bytes 3145744 | tf_op jit(solution)/shard_map/all_gather | solution.py:98
  369.9 15.3 %convolution_convert_fusion = bf16[1024,3072]{1,0:T(8,128)(2,1)} fusion(bf16[1024,1536]{0,1:T(8,128)(2,1)} %all-gather.11.cloned.1.call-done, bf16[1536,3072]{1,0:T(8,128)(2,1)} %bitcast.15), kind=kOutput, calls=%fused_computation.19 | convolution fusion | flops 9666822144 | bytes 18874368 | tf_op jit(solution)/shard_map/dot_general | solution.py:99
  385.2 65.3 %reduce-scatter.2.cloned.1.call-done = bf16[1024,768]{1,0:T(8,128)(2,1)} async-done(((bf16[1024,3072]{1,0:T(8,128)(2,1)}), bf16[1024,768]{1,0:T(8,128)(2,1)}) %reduce-scatter.2.cloned.1.call-update) | async-done | bytes 1572880 | tf_op jit(solution)/shard_map/reduce_scatter | solution.py:100
  450.5 6.5 %all_to_all.19 = bf16[2,512,768]{2,1,0:T(8,128)(2,1)S(1)} all-to-all(bf16[2,512,768]{2,1,0:T(8,128)(2,1)} %bitcast.56), channel_id=1, replica_groups=mesh['ylo'=2,'x'=4,'c'=2,'yhi'=2,'z'=4] {'c'}, dimensions={0} | all-to-all | bytes 3145728 | tf_op jit(solution)/shard_map/all_to_all | solution.py:101
  (100 shorter events, 39.2 us)
Async XLA Ops:
  6.5 5.6 %copy-start = (bf16[512,768]{1,0:T(8,128)(2,1)S(1)}, bf16[512,768]{1,0:T(8,128)(2,1)}, u32[]{:S(2)}) copy-start(bf16[512,768]{1,0:T(8,128)(2,1)} %param.8) | copy-start | bytes 2359300
  6.5 120.5 %all-gather.7.cloned.1.call-start = ((), (), s32[]{:S(2)}) async-start(), calls=%async_computation.5 | async-start | bytes 5898240 | tf_op jit(solution)/shard_map/all_gather | solution.py:69
  6.5 2.1 collective-permute-start
  8.6 1.0 copy-start.2
  9.6 167.0 %all-gather.5.cloned.1.call-start = ((), (), s32[]{:S(2)}) async-start(), calls=%async_computation.4 | async-start | bytes 4456448 | tf_op jit(solution)/shard_map/all_gather | solution.py:37
  16.3 119.0 %all-to-all-start = ((bf16[16,128,768]{2,1,0:T(8,128)(2,1)}), bf16[16,128,768]{2,1,0:T(8,128)(2,1)}, u32[]{:S(2)}, u32[]{:S(2)}) async-start(bf16[16,128,768]{2,1,0:T(8,128)(2,1)} %copy.10), calls=%async_computation | async-start | bytes 6291456 | tf_op jit(solution)/shard_map/all_to_all | solution.py:55
  135.3 7.5 %copy-start.5 = (s32[64,2]{0,1:T(2,128)S(1)}, s32[64,2]{0,1:T(2,128)}, u32[]{:S(2)}) copy-start(s32[64,2]{0,1:T(2,128)} %param.12) | copy-start | bytes 1540
  135.3 9.3 %copy-start.4 = (s32[8192]{0:T(1024)S(1)}, s32[8192]{0:T(1024)}, u32[]{:S(2)}) copy-start(s32[8192]{0:T(1024)} %param.11) | copy-start | bytes 98308
  135.3 125.7 %all-to-all-start.1 = ((bf16[2,768,3072]{2,1,0:T(8,128)(2,1)}), bf16[2,768,3072]{2,1,0:T(8,128)(2,1)}, u32[]{:S(2)}, u32[]{:S(2)}) async-start(bf16[2,768,3072]{2,1,0:T(8,128)(2,1)} %pad_maximum_fusion), calls=%async_computation.1 | async-start | bytes 18874368 | tf_op jit(solution)/shard_map/all_to_all | solution.py:71
  142.8 210.9 %all-gather.9.cloned.1.call-start = ((), (), s32[]{:S(2)}) async-start(), calls=%async_computation.6 | async-start | bytes 2359296 | tf_op jit(solution)/shard_map/all_gather | solution.py:97
  268.1 1.4 copy-start.3
  278.0 1.4 copy-start.3
  287.9 1.4 copy-start.3
  297.9 1.4 copy-start.3
  307.8 1.4 copy-start.3
  317.7 1.4 copy-start.3
  322.1 47.7 %all-gather.11.cloned.1.call-start = ((), (), s32[]{:S(2)}) async-start(), calls=%async_computation.7 | async-start | bytes 4718592 | tf_op jit(solution)/shard_map/all_gather | solution.py:98
  353.7 96.8 %reduce-scatter.2.cloned.1.call-start = ((), (), s32[]{:S(2)}) async-start(), calls=%async_computation.8 | async-start | bytes 7864320 | tf_op jit(solution)/shard_map/reduce_scatter | solution.py:100
  450.5 7.9 %copy-start.1 = (bf16[512,768]{1,0:T(8,128)(2,1)S(1)}, bf16[512,768]{1,0:T(8,128)(2,1)}, u32[]{:S(2)}) copy-start(bf16[512,768]{1,0:T(8,128)(2,1)} %param.8) | copy-start | bytes 2359300
Sparse Core Ops, SparseCore 0:
  9.8 117.2 all-gather.6
  128.7 47.8 all-gather.4
  322.3 31.3 all-gather.8
  355.2 14.6 all-gather.10
  385.4 65.1 reduce-scatter.1
